TPU v7x, 32 devices: a whole 2x2x4 slice. The times are simulated.
32 devices in a mesh: segment: 2 (over x), rows: 8 (over z, y), cols: 2 (over core).
Axes of the slice: x: 2, y: 2, z: 4, core: 2. Of those that a mesh axis runs over, the one named last changes fastest.
Arguments:
- frames: bfloat16 [2, 2, 16, 128, 128], P(None, None, 'rows', 'cols'), may hold values from -6 to 6
- cell_weight: bfloat16 [9, 256, 512], P(None, 'rows'), may hold values from -0.125 to 0.125
- cell_bias: float32 [512], replicated, may hold values from -3 to 3
- first_context_weight: bfloat16 [9, 128, 384], P(None, 'rows'), may hold values from -1 to 1
- first_context_bias: float32 [384], replicated, may hold values from -0.5 to 1
- second_context_weight: bfloat16 [9, 384, 384], P(None, 'rows'), may hold values from -0.109375 to 0.109375
- second_context_bias: float32 [384], replicated, may hold values from -0.5 to 1
- third_context_weight: bfloat16 [9, 384, 384], P(None, 'rows'), may hold values from -0.109375 to 0.109375
- third_context_bias: float32 [384], replicated, may hold values from 0 to 1
Outputs:
- context: bfloat16 [2, 16, 128, 384], P('segment', 'rows', 'cols')
All inputs are finite; a program needn't handle non-finite values.
Results may differ from a plain program's by a relative error of at most 0.0065.
Values may be sent and summed in bfloat16 or wider, within the bound.
A program may use at most 64 MiB of HBM per device.

v0:
```python
import jax
import jax.numpy as jnp
from jax import lax
from jax.sharding import PartitionSpec as P

FIRST_DILATION = 16
SECOND_DILATION = 32
THIRD_DILATION = 64


def extended(value, sides, width):
    for axis, dim in sides:
        devices, length = (lax.axis_size(axis), value.shape[dim])
        up = [(i, (i + 1) % devices) for i in range(devices - 1)]
        down = [(j, i) for i, j in up]
        last = lax.slice_in_dim(value, length - width, length, axis=dim)
        leading = lax.slice_in_dim(value, 0, width, axis=dim)
        before = lax.ppermute(last, axis, up)
        after = lax.ppermute(leading, axis, down)
        value = jnp.concatenate([before, value, after], axis=dim)
    return value


def shortened(value):

    def short(part):
        return part.astype(jnp.bfloat16) if part.dtype == jnp.float32 else part

    return jax.tree.map(short, value)


def from_behind(value, axis, steps):
    count = lax.axis_size(axis)
    leading, last = (max(0, -steps), min(count, count - steps))
    return lax.ppermute(value, axis, [(source, source + steps) for source in range(leading, last)])


def tap_product(tap_list, weight):
    stacked = jnp.concatenate(tap_list, axis=-1)
    height, across, channels = stacked.shape
    flattened = stacked.reshape(height * across, channels)
    product = jnp.dot(
        flattened, weight.reshape(channels, weight.shape[-1]), preferred_element_type=jnp.float32
    )
    return product.reshape(height, across, weight.shape[-1])


def cell_update(padded, memory, weight, offset):
    height, across, channels = memory.shape
    tap_list = [
        padded[row_tap : row_tap + height, col_tap : col_tap + across]
        for row_tap in range(3)
        for col_tap in range(3)
    ]
    gate_sums = tap_product(tap_list, weight) + offset
    inflow = jax.nn.sigmoid(gate_sums[..., :channels])
    forget = jax.nn.sigmoid(gate_sums[..., channels : 2 * channels])
    output = jax.nn.sigmoid(gate_sums[..., 2 * channels : 3 * channels])
    update = jnp.tanh(gate_sums[..., 3 * channels :])
    memory = forget * memory + inflow * update
    hidden_state = (output * jnp.tanh(memory)).astype(jnp.bfloat16)
    return (hidden_state, memory)


def cell_section(clip, weight, offset, active_mask):
    height, across = (clip.shape[1], clip.shape[2])
    channels = offset.shape[0] // 4
    hidden_state = jnp.zeros((height, across, channels), jnp.bfloat16)
    memory = jnp.zeros((height, across, channels), jnp.float32)

    def cell_compute(operands):
        return cell_update(operands[0], operands[1], weight, offset)

    def cell_skipped(operands):
        return (jnp.zeros((height, across, channels), jnp.bfloat16), jnp.zeros_like(operands[1]))

    for moment in range(clip.shape[0]):
        joined = jnp.concatenate([clip[moment], hidden_state], axis=-1)
        padded = extended(joined, (("rows", 0), ("cols", 1)), 1)
        hidden_state, memory = lax.cond(active_mask, cell_compute, cell_skipped, (padded, memory))
    return hidden_state


def dilated_context_layer(feature, weight, offset, spacing, active_mask):
    height, across = (feature.shape[0], feature.shape[1])
    widened = extended(feature, (("cols", 1),), spacing)
    reach = spacing // height
    groups = lax.axis_size("rows")
    if reach >= groups:
        before = jnp.zeros_like(widened)
        beyond = jnp.zeros_like(widened)
    else:
        before = from_behind(shortened(widened), "rows", reach).astype(widened.dtype)
        beyond = from_behind(shortened(widened), "rows", -reach).astype(widened.dtype)
    row_taps = [before, widened, beyond]
    tap_list = [
        row_taps[row_tap][:, col_tap * spacing : col_tap * spacing + across]
        for row_tap in range(3)
        for col_tap in range(3)
    ]

    def dilated_compute(pieces):
        return jnp.maximum(tap_product(pieces, weight) + offset, 0.0)

    def dilated_skipped(pieces):
        return jnp.zeros((height, across, weight.shape[-1]), jnp.float32)

    return lax.cond(active_mask, dilated_compute, dilated_skipped, tap_list)


def context_section(hidden_state, kernel_list, offset_list, active_mask):
    first_output = dilated_context_layer(
        hidden_state, kernel_list[0], offset_list[0], FIRST_DILATION, active_mask
    ).astype(jnp.bfloat16)
    second_output = dilated_context_layer(
        first_output, kernel_list[1], offset_list[1], SECOND_DILATION, active_mask
    ).astype(jnp.bfloat16)
    third_output = dilated_context_layer(
        second_output, kernel_list[2], offset_list[2], THIRD_DILATION, active_mask
    )
    return (second_output.astype(jnp.float32) + third_output).astype(jnp.bfloat16)


def per_device(
    frames,
    cell_weight,
    cell_bias,
    first_context_weight,
    first_context_bias,
    second_context_weight,
    second_context_bias,
    third_context_weight,
    third_context_bias,
):
    full_cell, full_first, full_second, full_third = (
        lax.all_gather(cell_weight, "rows", axis=1, tiled=True),
        lax.all_gather(first_context_weight, "rows", axis=1, tiled=True),
        lax.all_gather(second_context_weight, "rows", axis=1, tiled=True),
        lax.all_gather(third_context_weight, "rows", axis=1, tiled=True),
    )
    kernel_list = (full_first, full_second, full_third)
    offset_list = (first_context_bias, second_context_bias, third_context_bias)
    segment_index = lax.axis_index("segment")
    micro_count = frames.shape[0]
    half_count = micro_count // 2
    always = jnp.array(True)
    own_frames = lax.dynamic_slice_in_dim(frames, segment_index * half_count, half_count, 0)
    state = cell_section(own_frames[0], full_cell, cell_bias, always)
    results = [context_section(state, kernel_list, offset_list, always)]
    return jnp.stack(results)


def solution(mesh):
    placed = (
        P(None, None, "rows", "cols", None),
        P(None, "rows", None),
        P(),
        P(None, "rows", None),
        P(),
        P(None, "rows", None),
        P(),
        P(None, "rows", None),
        P(),
    )
    return jax.shard_map(
        per_device,
        mesh=mesh,
        in_specs=placed,
        out_specs=P("segment", "rows", "cols", None),
        check_vma=False,
    )
```

profile of v0, /device:TPU:0, one launch (start us, length us, event | category | flops | bytes accessed | tf_op | source)
XLA Modules:
  0.0 190.7 jit_solution(9595188403604663498)
XLA Ops:
  6.5 0.0 copy-start.1
  6.5 0.0 all-gather.4.cloned.1.call-start
  6.5 0.7 all-gather.4.cloned.1.call-update
  7.3 0.0 all-gather.6.cloned.1.call-start
  7.3 0.7 all-gather.6.cloned.1.call-update
  8.0 0.0 all-gather.8.cloned.1.call-start
  8.1 0.8 dynamic-slice_bitcast_fusion.1
  8.9 4.9 %collective-permute-start = (bf16[1,64,256]{2,1,0:T(8,128)(2,1)S(1)}, bf16[1,64,256]{2,1,0:T(8,128)(2,1)S(1)}, u32[]{:S(2)}, u32[]{:S(2)}) collective-permute-start(bf16[1,64,256]{2,1,0:T(8,128)(2,1)S(1)} %get-tuple-element.23), channel_id=1, source_target_pairs={{0,2},{2,4},{4,6},{6,8},{8,10},{10,12},{12,14},{1,3},{3,5},{5,7},{... | collective-permute-start | bytes 98312 | tf_op jit(solution)/shard_map/ppermute | solution.py:18
  13.8 1.3 collective-permute-start.1
  15.1 0.0 all-gather.8.cloned.1.call-update
  15.1 36.8 %all_gather.13 = bf16[9,128,384]{2,1,0:T(8,128)(2,1)S(1)} all-gather(bf16[9,16,384]{2,1,0:T(8,128)(2,1)} %param.12), channel_id=1, replica_groups=mesh['segment'=2,'rows'=8,'cols'=2] {'rows'}, dimensions={1}, use_global_device_ids=true | all-gather | bytes 995328 | tf_op jit(solution)/shard_map/all_gather | solution.py:137
  51.9 0.0 collective-permute-done
  51.9 0.0 collective-permute-done.1
  52.0 1.3 collective-permute-start.2
  53.3 1.3 collective-permute-start.3
  54.6 0.0 collective-permute-done.2
  54.6 1.7 collective-permute-done.3
  56.3 0.1 pad_maximum_fusion
  56.6 12.3 %all-gather.4.cloned.1.call-done = bf16[9,256,512]{2,1,0:T(8,128)(2,1)} async-done(((bf16[9,32,512]{2,1,0:T(8,128)(2,1)}), bf16[9,256,512]{2,1,0:T(8,128)(2,1)}) %all-gather.4.cloned.1.call-update) | async-done | bytes 2359312 | tf_op jit(solution)/shard_map/all_gather | solution.py:136
  68.9 0.0 copy-done.1
  68.9 0.0 copy-start
  68.9 2.3 %convolution_add_fusion.1 = f32[2,64,512]{2,1,0:T(8,128)S(1)} fusion(bf16[2,64,2304]{2,1,0:T(8,128)(2,1)S(1)} %constant_dynamic-update-slice_fusion, bf16[2304,512,1]{1,0,2:T(8,128)(2,1)} %bitcast.28, f32[512]{0:T(512)S(1)} %copy-done.1), kind=kOutput, calls=%fused_computation.1 | convolution fusion | flops 302055424 | bytes 3213312 | tf_op jit(solution)/shard_map/cond/branch_1_fun/dot_general | solution.py:42
  71.2 0.1 fusion.38
  71.3 3.4 %collective-permute-start.4 = (bf16[1,64,256]{2,1,0:T(8,128)(2,1)S(1)}, bf16[1,64,256]{2,1,0:T(8,128)(2,1)S(1)}, u32[]{:S(2)}, u32[]{:S(2)}) collective-permute-start(bf16[1,64,256]{2,1,0:T(8,128)(2,1)S(1)} %get-tuple-element.19), channel_id=1, source_target_pairs={{0,2},{2,4},{4,6},{6,8},{8,10},{10,12},{12,14},{1,3},{3,5},{5,7},{... | collective-permute-start | bytes 98312 | tf_op jit(solution)/shard_map/ppermute | solution.py:18
  74.7 1.3 collective-permute-start.5
  76.0 0.3 collective-permute-done.4
  76.3 4.2 %collective-permute-done.5 = bf16[1,64,256]{2,1,0:T(8,128)(2,1)S(1)} collective-permute-done((bf16[1,64,256]{2,1,0:T(8,128)(2,1)S(1)}, bf16[1,64,256]{2,1,0:T(8,128)(2,1)S(1)}, u32[]{:S(2)}, u32[]{:S(2)}) %collective-permute-start.5) | collective-permute-done | bytes 32800 | tf_op jit(solution)/shard_map/ppermute | solution.py:19
  80.5 1.3 collective-permute-start.6
  81.8 1.3 collective-permute-start.7
  83.1 0.0 collective-permute-done.6
  83.1 1.7 collective-permute-done.7
  84.9 0.1 pad_maximum_fusion.1
  84.9 0.0 copy-start.4
  85.1 0.0 copy-done
  85.1 0.0 copy-start.3
  85.1 0.5 convolution_add_fusion
  85.6 0.1 fusion.14
  85.7 2.1 %collective-permute-start.8 = (bf16[2,16,128]{2,1,0:T(8,128)(2,1)S(1)}, bf16[2,16,128]{2,1,0:T(8,128)(2,1)S(1)}, u32[]{:S(2)}, u32[]{:S(2)}) collective-permute-start(bf16[2,16,128]{2,1,0:T(8,128)(2,1)S(1)} %get-tuple-element.22), channel_id=1, source_target_pairs={{0,1},{2,3},{4,5},{6,7},{8,9},{10,11},{12,13},{14,15},{16,17},{18,... | collective-permute-start | bytes 24584 | tf_op jit(solution)/shard_map/ppermute | solution.py:18
  87.8 1.3 collective-permute-start.9
  89.1 0.0 collective-permute-done.8
  89.2 1.7 collective-permute-done.9
  90.9 0.0 copy-done.4
  91.0 0.3 fusion.4
  91.3 2.1 %collective-permute-start.10 = (bf16[2,32,384]{2,1,0:T(8,128)(2,1)S(1)}, bf16[2,32,384]{2,1,0:T(8,128)(2,1)S(1)}, u32[]{:S(2)}, u32[]{:S(2)}) collective-permute-start(bf16[2,32,384]{2,1,0:T(8,128)(2,1)S(1)} %get-tuple-element.18), channel_id=1, source_target_pairs={{0,1},{2,3},{4,5},{6,7},{8,9},{10,11},{12,13},{14,15},{16,17},{18,... | collective-permute-start | bytes 147464 | tf_op jit(solution)/shard_map/ppermute | solution.py:18
  93.4 1.3 collective-permute-start.11
  94.7 0.0 collective-permute-done.10
  94.8 1.8 collective-permute-done.11
  96.6 29.0 %all-gather.6.cloned.1.call-done = bf16[9,384,384]{2,1,0:T(8,128)(2,1)} async-done(((bf16[9,48,384]{2,1,0:T(8,128)(2,1)}), bf16[9,384,384]{2,1,0:T(8,128)(2,1)}) %all-gather.6.cloned.1.call-update) | async-done | bytes 2654224 | tf_op jit(solution)/shard_map/all_gather | solution.py:138
  125.5 0.0 copy-done.3
  125.5 0.0 copy-start.2
  125.5 2.4 %fusion.5 = bf16[2,64,384]{2,1,0:T(8,128)(2,1)S(1)} fusion(bf16[2,64,3456]{2,1,0:T(8,128)(2,1)S(1)} %constant_dynamic-update-slice_fusion.27, bf16[3456,384,1]{1,0,2:T(8,128)(2,1)} %bitcast.30, f32[384]{0:T(512)S(1)} %copy-done.3), kind=kOutput, calls=%fused_computation.10 | convolution fusion | flops 339886080 | bytes 3638784 | tf_op jit(solution)/shard_map/cond/branch_1_fun/dot_general | solution.py:42
  128.0 1.3 collective-permute-start.12
  129.3 1.3 collective-permute-start.13
  130.6 0.0 collective-permute-done.12
  130.6 1.8 collective-permute-done.13
  132.5 48.6 %all-gather.8.cloned.1.call-done = bf16[9,384,384]{2,1,0:T(8,128)(2,1)} async-done(((bf16[9,48,384]{2,1,0:T(8,128)(2,1)}), bf16[9,384,384]{2,1,0:T(8,128)(2,1)}) %all-gather.8.cloned.1.call-update) | async-done | bytes 2654224 | tf_op jit(solution)/shard_map/all_gather | solution.py:139
  181.2 0.0 copy-done.2
  181.2 3.0 %fusion.7 = bf16[1,2,64,384]{3,2,1,0:T(8,128)(2,1)} fusion(bf16[2,64,3456]{2,1,0:T(8,128)(2,1)S(1)} %constant_dynamic-update-slice_fusion.30, bf16[3456,384,1]{1,0,2:T(8,128)(2,1)} %bitcast.32, bf16[2,64,384]{2,1,0:T(8,128)(2,1)S(1)} %fusion.5, f32[384]{0:T(512)S(1)} %copy-done.2), kind=kOutput, calls=%fused_computation.12 | convolution fusion | flops 339984384 | bytes 3737088 | tf_op jit(solution)/shard_map/cond/branch_1_fun/dot_general | solution.py:42
  (48 shorter events, 0.6 us)
Async XLA Ops:
  6.5 62.3 %copy-start.1 = (f32[512]{0:T(512)S(1)}, f32[512]{0:T(512)}, u32[]{:S(2)}) copy-start(f32[512]{0:T(512)} %param.11) | copy-start | bytes 6148
  6.5 62.3 %all-gather.4.cloned.1.call-start = ((), (), s32[]{:S(2)}) async-start(), calls=%async_computation | async-start | bytes 2654208 | tf_op jit(solution)/shard_map/all_gather | solution.py:136
  7.3 118.3 %all-gather.6.cloned.1.call-start = ((), (), s32[]{:S(2)}) async-start(), calls=%async_computation.1 | async-start | bytes 2985984 | tf_op jit(solution)/shard_map/all_gather | solution.py:138
  8.0 173.2 %all-gather.8.cloned.1.call-start = ((), (), s32[]{:S(2)}) async-start(), calls=%async_computation.2 | async-start | bytes 2985984 | tf_op jit(solution)/shard_map/all_gather | solution.py:139
  8.9 43.1 %collective-permute-start = (bf16[1,64,256]{2,1,0:T(8,128)(2,1)S(1)}, bf16[1,64,256]{2,1,0:T(8,128)(2,1)S(1)}, u32[]{:S(2)}, u32[]{:S(2)}) collective-permute-start(bf16[1,64,256]{2,1,0:T(8,128)(2,1)S(1)} %get-tuple-element.23), channel_id=1, source_target_pairs={{0,2},{2,4},{4,6},{6,8},{8,10},{10,12},{12,14},{1,3},{3,5},{5,7},{... | collective-permute-start | bytes 98312 | tf_op jit(solution)/shard_map/ppermute | solution.py:18
  13.8 38.2 %collective-permute-start.1 = (bf16[1,64,256]{2,1,0:T(8,128)(2,1)S(1)}, bf16[1,64,256]{2,1,0:T(8,128)(2,1)S(1)}, u32[]{:S(2)}, u32[]{:S(2)}) collective-permute-start(bf16[1,64,256]{2,1,0:T(8,128)(2,1)S(1)} %get-tuple-element.24), channel_id=1, source_target_pairs={{2,0},{4,2},{6,4},{8,6},{10,8},{12,10},{14,12},{3,1},{5,3},{7,5},{... | collective-permute-start | bytes 98312 | tf_op jit(solution)/shard_map/ppermute | solution.py:19
  52.0 2.6 %collective-permute-start.2 = (bf16[4,1,256]{2,1,0:T(2,128)(2,1)S(1)}, bf16[4,1,256]{2,1,0:T(2,128)(2,1)S(1)}, u32[]{:S(2)}, u32[]{:S(2)}) collective-permute-start(bf16[4,1,256]{2,1,0:T(2,128)(2,1)S(1)} %get-tuple-element.16), channel_id=1, source_target_pairs={{0,1},{2,3},{4,5},{6,7},{8,9},{10,11},{12,13},{14,15},{16,17},{18,... | collective-permute-start | bytes 6152 | tf_op jit(solution)/shard_map/ppermute | solution.py:18
  53.3 3.1 %collective-permute-start.3 = (bf16[4,1,256]{2,1,0:T(2,128)(2,1)S(1)}, bf16[4,1,256]{2,1,0:T(2,128)(2,1)S(1)}, u32[]{:S(2)}, u32[]{:S(2)}) collective-permute-start(bf16[4,1,256]{2,1,0:T(2,128)(2,1)S(1)} %get-tuple-element.15), channel_id=1, source_target_pairs={{1,0},{3,2},{5,4},{7,6},{9,8},{11,10},{13,12},{15,14},{17,16},{19,... | collective-permute-start | bytes 6152 | tf_op jit(solution)/shard_map/ppermute | solution.py:19
  68.9 16.2 %copy-start = (bf16[9,256,512]{2,1,0:T(8,128)(2,1)S(1)}, bf16[9,256,512]{2,1,0:T(8,128)(2,1)}, u32[]{:S(2)}) copy-start(bf16[9,256,512]{2,1,0:T(8,128)(2,1)} %all-gather.4.cloned.1.call-done) | copy-start | bytes 7077892
  71.3 5.0 %collective-permute-start.4 = (bf16[1,64,256]{2,1,0:T(8,128)(2,1)S(1)}, bf16[1,64,256]{2,1,0:T(8,128)(2,1)S(1)}, u32[]{:S(2)}, u32[]{:S(2)}) collective-permute-start(bf16[1,64,256]{2,1,0:T(8,128)(2,1)S(1)} %get-tuple-element.19), channel_id=1, source_target_pairs={{0,2},{2,4},{4,6},{6,8},{8,10},{10,12},{12,14},{1,3},{3,5},{5,7},{... | collective-permute-start | bytes 98312 | tf_op jit(solution)/shard_map/ppermute | solution.py:18
  74.7 5.8 %collective-permute-start.5 = (bf16[1,64,256]{2,1,0:T(8,128)(2,1)S(1)}, bf16[1,64,256]{2,1,0:T(8,128)(2,1)S(1)}, u32[]{:S(2)}, u32[]{:S(2)}) collective-permute-start(bf16[1,64,256]{2,1,0:T(8,128)(2,1)S(1)} %get-tuple-element.20), channel_id=1, source_target_pairs={{2,0},{4,2},{6,4},{8,6},{10,8},{12,10},{14,12},{3,1},{5,3},{7,5},{... | collective-permute-start | bytes 98312 | tf_op jit(solution)/shard_map/ppermute | solution.py:19
  80.5 2.6 %collective-permute-start.6 = (bf16[4,1,256]{2,1,0:T(2,128)(2,1)S(1)}, bf16[4,1,256]{2,1,0:T(2,128)(2,1)S(1)}, u32[]{:S(2)}, u32[]{:S(2)}) collective-permute-start(bf16[4,1,256]{2,1,0:T(2,128)(2,1)S(1)} %get-tuple-element.10), channel_id=1, source_target_pairs={{0,1},{2,3},{4,5},{6,7},{8,9},{10,11},{12,13},{14,15},{16,17},{18,... | collective-permute-start | bytes 6152 | tf_op jit(solution)/shard_map/ppermute | solution.py:18
  81.8 3.1 %collective-permute-start.7 = (bf16[4,1,256]{2,1,0:T(2,128)(2,1)S(1)}, bf16[4,1,256]{2,1,0:T(2,128)(2,1)S(1)}, u32[]{:S(2)}, u32[]{:S(2)}) collective-permute-start(bf16[4,1,256]{2,1,0:T(2,128)(2,1)S(1)} %get-tuple-element.9), channel_id=1, source_target_pairs={{1,0},{3,2},{5,4},{7,6},{9,8},{11,10},{13,12},{15,14},{17,16},{19,... | collective-permute-start | bytes 6152 | tf_op jit(solution)/shard_map/ppermute | solution.py:19
  84.9 6.0 %copy-start.4 = (f32[384]{0:T(512)S(1)}, f32[384]{0:T(512)}, u32[]{:S(2)}) copy-start(f32[384]{0:T(512)} %param.13) | copy-start | bytes 4612
  85.1 40.4 %copy-start.3 = (f32[384]{0:T(512)S(1)}, f32[384]{0:T(512)}, u32[]{:S(2)}) copy-start(f32[384]{0:T(512)} %param.15) | copy-start | bytes 4612
  85.7 3.4 %collective-permute-start.8 = (bf16[2,16,128]{2,1,0:T(8,128)(2,1)S(1)}, bf16[2,16,128]{2,1,0:T(8,128)(2,1)S(1)}, u32[]{:S(2)}, u32[]{:S(2)}) collective-permute-start(bf16[2,16,128]{2,1,0:T(8,128)(2,1)S(1)} %get-tuple-element.22), channel_id=1, source_target_pairs={{0,1},{2,3},{4,5},{6,7},{8,9},{10,11},{12,13},{14,15},{16,17},{18,... | collective-permute-start | bytes 24584 | tf_op jit(solution)/shard_map/ppermute | solution.py:18
  87.8 3.1 %collective-permute-start.9 = (bf16[2,16,128]{2,1,0:T(8,128)(2,1)S(1)}, bf16[2,16,128]{2,1,0:T(8,128)(2,1)S(1)}, u32[]{:S(2)}, u32[]{:S(2)}) collective-permute-start(bf16[2,16,128]{2,1,0:T(8,128)(2,1)S(1)} %get-tuple-element.21), channel_id=1, source_target_pairs={{1,0},{3,2},{5,4},{7,6},{9,8},{11,10},{13,12},{15,14},{17,16},{19,... | collective-permute-start | bytes 24584 | tf_op jit(solution)/shard_map/ppermute | solution.py:19
  91.3 3.4 %collective-permute-start.10 = (bf16[2,32,384]{2,1,0:T(8,128)(2,1)S(1)}, bf16[2,32,384]{2,1,0:T(8,128)(2,1)S(1)}, u32[]{:S(2)}, u32[]{:S(2)}) collective-permute-start(bf16[2,32,384]{2,1,0:T(8,128)(2,1)S(1)} %get-tuple-element.18), channel_id=1, source_target_pairs={{0,1},{2,3},{4,5},{6,7},{8,9},{10,11},{12,13},{14,15},{16,17},{18,... | collective-permute-start | bytes 147464 | tf_op jit(solution)/shard_map/ppermute | solution.py:18
  93.4 3.1 %collective-permute-start.11 = (bf16[2,32,384]{2,1,0:T(8,128)(2,1)S(1)}, bf16[2,32,384]{2,1,0:T(8,128)(2,1)S(1)}, u32[]{:S(2)}, u32[]{:S(2)}) collective-permute-start(bf16[2,32,384]{2,1,0:T(8,128)(2,1)S(1)} %get-tuple-element.17), channel_id=1, source_target_pairs={{1,0},{3,2},{5,4},{7,6},{9,8},{11,10},{13,12},{15,14},{17,16},{19,... | collective-permute-start | bytes 147464 | tf_op jit(solution)/shard_map/ppermute | solution.py:19
  125.5 55.6 %copy-start.2 = (f32[384]{0:T(512)S(1)}, f32[384]{0:T(512)}, u32[]{:S(2)}) copy-start(f32[384]{0:T(512)} %param.17) | copy-start | bytes 4612
  128.0 2.6 %collective-permute-start.12 = (bf16[2,64,384]{2,1,0:T(8,128)(2,1)S(1)}, bf16[2,64,384]{2,1,0:T(8,128)(2,1)S(1)}, u32[]{:S(2)}, u32[]{:S(2)}) collective-permute-start(bf16[2,64,384]{2,1,0:T(8,128)(2,1)S(1)} %fusion.5), channel_id=1, source_target_pairs={{0,1},{2,3},{4,5},{6,7},{8,9},{10,11},{12,13},{14,15},{16,17},{18,... | collective-permute-start | bytes 294920 | tf_op jit(solution)/shard_map/ppermute | solution.py:18
  129.3 3.2 %collective-permute-start.13 = (bf16[2,64,384]{2,1,0:T(8,128)(2,1)S(1)}, bf16[2,64,384]{2,1,0:T(8,128)(2,1)S(1)}, u32[]{:S(2)}, u32[]{:S(2)}) collective-permute-start(bf16[2,64,384]{2,1,0:T(8,128)(2,1)S(1)} %fusion.5), channel_id=1, source_target_pairs={{1,0},{3,2},{5,4},{7,6},{9,8},{11,10},{13,12},{15,14},{17,16},{19,... | collective-permute-start | bytes 294920 | tf_op jit(solution)/shard_map/ppermute | solution.py:19
Sparse Core Ops, SparseCore 0:
  9.5 59.3 all-gather.3
  71.1 54.3 all-gather.5
  127.8 53.3 all-gather.7
where the time goes:
time: 191 us
  waiting for transfers between devices  105 us (55%)
  blocking collectives  36.8 us (19%)
  starting transfers between devices  25.4 us (13%)
  between operations  13.7 us (7%)
  matrix products  8.51 us (4%)
    all_gather x1, waiting for transfers between devices, per_device(): lax.all_gather(third_context_weight, 'rows', axis=1, tiled=True)  48.6 us
    all_gather x1, blocking collectives, per_device(): lax.all_gather(first_context_weight, 'rows', axis=1, tiled=True)  36.8 us
    all_gather x1, waiting for transfers between devices, per_device(): lax.all_gather(second_context_weight, 'rows', axis=1, tiled=True)  29 us
    ppermute x7, starting transfers between devices, extended(): before = lax.ppermute(last, axis, up)  16.3 us
    ppermute x7, waiting for transfers between devices, extended(): after = lax.ppermute(leading, axis, down)  13 us
    all_gather x1, waiting for transfers between devices, per_device(): lax.all_gather(cell_weight, 'rows', axis=1, tiled=True)  12.3 us
    ppermute x7, starting transfers between devices, extended(): after = lax.ppermute(leading, axis, down)  9.04 us
    dot_general x5, matrix products, tap_product(): jnp.dot(flattened, weight.reshape(channels, weight.shape[-1]), preferred_...  8.51 us
  transfers between devices with their start and end apart: 17, of which 10 were waited for; matrix products, arithmetic and copies ran while one was open for 4% of the time, Pallas kernels for 0%

commit v1 on v0

v1 whole, which is shorter than its diff:
```python
import jax
import jax.numpy as jnp
from jax import lax
from jax.experimental import pallas as pl
from jax.experimental.pallas import tpu as pltpu
from jax.sharding import PartitionSpec as P

DILATIONS = (16, 32, 64)
MESH_ID = pl.DeviceIdType.MESH
MARGIN = 16


def encoder_kernel(
    frames, cell_w, cell_b, first_w, first_b, second_w, second_b, third_w, third_b,
    out, wc, w1, w2, w3, fp, hp, f1, f2, f3,
    local_sem, ring_s, ring_r, pair_s, pair_r, ex_s, ex_r, *, n, cols, row_pads,
):
    seg, r, c = lax.axis_index("segment"), lax.axis_index("rows"), lax.axis_index("cols")
    steps, height, across, channels = frames.shape[1:]
    state = cell_b.shape[-1] // 4
    half = n // 2
    odd = c % 2
    even_core, odd_core = odd == 0, odd == 1
    sign = 1 - 2 * odd
    parity = r % 2
    place = (1 - parity) * (r // 2) + parity * (n - 1 - r // 2)

    def rows_at(position):
        upper = position // half
        return (1 - upper) * 2 * position + upper * (2 * (n - 1 - position) + 1)

    following = rows_at((place + sign + n) % n)
    preceding = rows_at((place - sign + n) % n)
    partner = c + 1 - 2 * odd
    ahead_id, partner_id = (seg, following, c), (seg, r, partner)

    reaches = sorted({1} | {s // height for s, pad in zip(DILATIONS, row_pads) if pad})
    offsets = [(0, -1), (0, 1)] + [
        (d * reach, dc) for reach in reaches for d in (-1, 1) for dc in (-1, 0, 1)
    ]

    def present(dr, dc):
        row, col = r + dr, c + dc
        return jnp.logical_and(
            jnp.logical_and(row >= 0, row < n), jnp.logical_and(col >= 0, col < cols)
        )

    locals_ = []
    for t in range(steps):
        locals_.append(
            pltpu.make_async_copy(
                frames.at[seg, t],
                fp.at[t, pl.ds(1, height), pl.ds(MARGIN, across)],
                local_sem.at[t],
            )
        )
    stored = (cell_w, first_w, second_w, third_w)
    gathered = (wc, w1, w2, w3)
    own = []
    for ref, whole in zip(stored, gathered):
        taps = whole.shape[1]
        own.append(ref.at[pl.ds((9 - taps) // 2, taps)])
    for a in range(4):
        locals_.append(
            pltpu.make_async_copy(own[a], gathered[a].at[r], local_sem.at[steps + a])
        )
    for t in range(steps):
        fp[t] = jnp.zeros(fp.shape[1:], fp.dtype)
    for t in range(hp.shape[0]):
        hp[t] = jnp.zeros(hp.shape[1:], hp.dtype)
    for buffer in (f1, f2, f3):
        buffer[...] = jnp.zeros(buffer.shape, buffer.dtype)
    for copy in locals_:
        copy.start()

    barrier = pltpu.get_barrier_semaphore()
    expected = jnp.int32(2)
    for target in (following, preceding):
        pl.semaphore_signal(barrier, inc=1, device_id=(seg, target, c), device_id_type=MESH_ID)
    for dr, dc in offsets:
        there = present(dr, dc)
        expected = expected + there.astype(jnp.int32)

        @pl.when(there)
        def _():
            pl.semaphore_signal(
                barrier, inc=1, device_id=(seg, r + dr, c + dc), device_id_type=MESH_ID
            )

    pl.semaphore_wait(barrier, expected)

    def exchange(number, source_of, buffer, pad, reach, width):
        arrivals, departures = [], []
        for i, (dr, dc) in enumerate((a, b) for a in (-1, 0, 1) for b in (-1, 0, 1)):
            if (dr, dc) == (0, 0) or (dr and not pad):
                continue
            first, span, landing = {
                -1: (0, pad, pad + height), 0: (0, height, pad), 1: (height - pad, pad, 0)
            }[dr]
            left, extent, side = {
                -1: (0, width[1], width[0] + across),
                0: (0, across, width[0]),
                1: (across - width[1], width[1], width[0] - width[1]),
            }[dc]
            copy = pltpu.make_async_remote_copy(
                src_ref=source_of(first, span, left, extent),
                dst_ref=buffer.at[pl.ds(landing, span), pl.ds(side, extent)],
                send_sem=ex_s.at[number, i],
                recv_sem=ex_r.at[number, i],
                device_id=(seg, r + dr * reach, c + dc),
                device_id_type=MESH_ID,
            )
            there, behind = present(dr * reach, dc), present(-dr * reach, -dc)
            pl.when(there)(copy.start)
            departures.append((there, copy))
            arrivals.append((behind, copy))

        def arrive():
            for behind, copy in arrivals:
                pl.when(behind)(copy.wait_recv)

        def depart():
            for there, copy in departures:
                pl.when(there)(copy.wait_send)

        return arrive, depart

    def block_of(buffer, pad, margin):
        return lambda first, span, left, extent: buffer.at[
            pl.ds(pad + first, span), pl.ds(margin + left, extent)
        ]

    departs = []
    frame_arrivals = []
    for t in range(steps):
        arrive, depart = exchange(
            t,
            lambda first, span, left, extent, t=t: frames.at[
                seg, t, pl.ds(first, span), pl.ds(left, extent)
            ],
            fp.at[t], 1, 1, (MARGIN, MARGIN),
        )
        frame_arrivals.append(arrive)
        departs.append(depart)

    def ring_copy(a, k):
        slot = gathered[a].at[rows_at((place - sign * k + n) % n)]
        return pltpu.make_async_remote_copy(
            src_ref=own[a] if k == 0 else slot,
            dst_ref=slot,
            send_sem=ring_s.at[a, k],
            recv_sem=ring_r.at[a, k],
            device_id=ahead_id,
            device_id_type=MESH_ID,
        )

    def arriving(a, k):
        slot = gathered[a].at[rows_at((place - sign * k + n) % n)]
        return pltpu.make_async_remote_copy(
            src_ref=slot, dst_ref=slot, send_sem=ring_s.at[a, k - 1],
            recv_sem=ring_r.at[a, k - 1], device_id=ahead_id, device_id_type=MESH_ID,
        )

    def pair_copy(a, k, direction):
        slot = gathered[a].at[rows_at((place - direction * sign * k + n) % n)]
        return pltpu.make_async_remote_copy(
            src_ref=slot, dst_ref=slot, send_sem=pair_s.at[a, k], recv_sem=pair_r.at[a, k],
            device_id=partner_id, device_id_type=MESH_ID,
        )

    def longer(a):
        return even_core if a == 0 else odd_core

    def guarded(condition, act):
        if condition is None:
            act()
        else:
            pl.when(condition)(act)

    def ring_send(a, k):
        guarded(longer(a) if k == half - 1 else None, ring_copy(a, k).start)

    def ring_step(a, k):
        def act():
            arriving(a, k).wait_recv()
            if k < half:
                ring_send(a, k)
            pair_copy(a, k, 1).start()

        guarded(longer(a) if k == half else None, act)

    def pair_waits(a):
        for k in range(1, half + 1):
            shorter = odd_core if a == 0 else even_core
            guarded(shorter if k == half else None, pair_copy(a, k, -1).wait_recv)

    ring_send(0, 0)
    for k in range(1, half + 1):
        ring_step(0, k)
        if k <= 3:
            ring_send(k, 0)
    for k in range(half + 1, 4):
        ring_send(k, 0)

    for copy in locals_:
        copy.wait()
    for arrive in frame_arrivals:
        arrive()
    pair_waits(0)

    bias = cell_b[...]
    per = wc.shape[2]
    frame_sources = channels // per

    def tap_columns(buffer):
        taps = []
        for row in range(height + 2):
            wide = buffer[row].astype(jnp.float32)
            length = wide.shape[0]
            taps.append(
                [
                    pltpu.roll(wide, 1, 0)[MARGIN : MARGIN + across].astype(jnp.bfloat16),
                    buffer[row, MARGIN : MARGIN + across],
                    pltpu.roll(wide, length - 1, 0)[MARGIN : MARGIN + across].astype(
                        jnp.bfloat16
                    ),
                ]
            )
        return taps

    def gate_part(buffer, sources):
        taps = tap_columns(buffer)
        left = jnp.concatenate(
            [
                jnp.concatenate([taps[row + a][b] for row in range(height)], axis=0)
                for a in range(3)
                for b in range(3)
            ],
            axis=1,
        )
        right = jnp.concatenate([wc[s, t] for t in range(9) for s in sources], axis=0)
        return jnp.dot(left, right, preferred_element_type=jnp.float32)

    def update(gates, memory):
        inflow = jax.nn.sigmoid(gates[:, :state])
        forget = jax.nn.sigmoid(gates[:, state : 2 * state])
        output = jax.nn.sigmoid(gates[:, 2 * state : 3 * state])
        fresh = inflow * jnp.tanh(gates[:, 3 * state :])
        memory = fresh if memory is None else forget * memory + fresh
        return (output * jnp.tanh(memory)).astype(jnp.bfloat16), memory

    context_steps = list(range(1, half + 1))
    quarter = max(1, half // 4)

    def context_ring(count):
        for _ in range(min(count, len(context_steps))):
            k = context_steps.pop(0)
            for a in (1, 2, 3):
                ring_step(a, k)

    seen, unseen = range(frame_sources), range(frame_sources, n)
    hidden, memory = update(gate_part(fp.at[0], seen) + bias, None)
    for t in range(1, steps):
        view = hp.at[t - 1]
        for row in range(height):
            view[1 + row, MARGIN : MARGIN + across] = hidden[row * across : (row + 1) * across]
        arrive, depart = exchange(
            steps + t - 1, block_of(view, 1, MARGIN), view, 1, 1, (MARGIN, MARGIN)
        )
        departs.append(depart)
        context_ring(quarter)
        gates = gate_part(fp.at[t], seen) + bias
        context_ring(quarter)
        arrive()
        hidden, memory = update(gates + gate_part(view, unseen), memory)

    feature = hidden
    layers = ((f1, w1, first_b), (f2, w2, second_b), (f3, w3, third_b))
    for i, (buffer, weight, offset) in enumerate(layers):
        spacing, pad = DILATIONS[i], row_pads[i]
        for row in range(height):
            buffer[pad + row, spacing : spacing + across] = feature[
                row * across : (row + 1) * across
            ]
        arrive, depart = exchange(
            2 * steps - 1 + i, block_of(buffer, pad, spacing), buffer, pad,
            spacing // height, (spacing, spacing),
        )
        departs.append(depart)
        if i == 0:
            context_ring(len(context_steps))
        pair_waits(i + 1)
        arrive()
        total = None
        taps = weight.shape[1]
        for t in range(taps):
            a, b = t // 3, t % 3
            left = buffer[a * pad : a * pad + height, b * spacing : b * spacing + across]
            left = left.reshape(height * across, left.shape[-1])
            right = jnp.concatenate([weight[s, t] for s in range(n)], axis=0)
            product = jnp.dot(left, right, preferred_element_type=jnp.float32)
            total = product if total is None else total + product
        result = jnp.maximum(total + offset[...], 0.0)
        if i < 2:
            feature = result.astype(jnp.bfloat16)
    context = (feature.astype(jnp.float32) + result).astype(jnp.bfloat16)
    out[0] = context.reshape(out.shape[1:])

    for depart in departs:
        depart()
    for a in range(4):
        for k in range(half):
            guarded(longer(a) if k == half - 1 else None, ring_copy(a, k).wait_send)
        for k in range(1, half + 1):
            guarded(longer(a) if k == half else None, pair_copy(a, k, 1).wait_send)


def per_device(n, cols, *args):
    import functools

    frames, cell_w, cell_b, first_w, first_b, second_w, second_b, third_w, third_b = args
    micro, steps, height, across, channels = frames.shape
    state, width = cell_b.shape[0] // 4, first_b.shape[0]
    row_pads = tuple(height if s // height < n else 0 for s in DILATIONS)

    def slots(weight, pad):
        return pltpu.VMEM((n, 9 if pad else 3) + weight.shape[1:], weight.dtype)

    def field(spacing, pad, depth):
        return pltpu.VMEM((height + 2 * pad, across + 2 * spacing, depth), jnp.bfloat16)

    half = n // 2
    exchanges = 2 * steps - 1 + 3
    dma = pltpu.SemaphoreType.DMA
    anywhere, vmem = pl.BlockSpec(memory_space=pl.ANY), pl.BlockSpec(memory_space=pltpu.VMEM)
    return pl.pallas_call(
        functools.partial(encoder_kernel, n=n, cols=cols, row_pads=row_pads),
        out_shape=jax.ShapeDtypeStruct((1, height, across, width), jnp.bfloat16),
        in_specs=[anywhere, anywhere, vmem, anywhere, vmem, anywhere, vmem, anywhere, vmem],
        out_specs=vmem,
        scratch_shapes=[
            slots(cell_w, 1),
            slots(first_w, row_pads[0]),
            slots(second_w, row_pads[1]),
            slots(third_w, row_pads[2]),
            pltpu.VMEM((steps, height + 2, across + 2 * MARGIN, channels), jnp.bfloat16),
            pltpu.VMEM((steps - 1, height + 2, across + 2 * MARGIN, state), jnp.bfloat16),
            field(DILATIONS[0], row_pads[0], state),
            field(DILATIONS[1], row_pads[1], width),
            field(DILATIONS[2], row_pads[2], width),
            dma((steps + 4,)),
            dma((4, half)),
            dma((4, half)),
            dma((4, half + 1)),
            dma((4, half + 1)),
            dma((exchanges, 9)),
            dma((exchanges, 9)),
        ],
        compiler_params=pltpu.CompilerParams(collective_id=0, has_side_effects=True),
    )(
        frames, cell_w, cell_b[None], first_w, first_b[None], second_w, second_b[None],
        third_w, third_b[None],
    )


def solution(mesh):
    import functools

    kernels = P(None, "rows", None)
    placed = (
        P(None, None, "rows", "cols", None),
        kernels, P(), kernels, P(), kernels, P(), kernels, P(),
    )
    return jax.shard_map(
        functools.partial(per_device, mesh.shape["rows"], mesh.shape["cols"]),
        mesh=mesh,
        in_specs=placed,
        out_specs=P("segment", "rows", "cols", None),
        check_vma=False,
    )
```

time: 191 us -> 50 us (0.26)
  waiting for transfers between devices: 105 us -> 0 us
  Pallas kernels: 0 us -> 45.4 us
  blocking collectives: 36.8 us -> 0 us
  starting transfers between devices: 25.4 us -> 0 us
  between operations: 13.7 us -> 0.01 us
  matrix products: 8.51 us -> 0 us
  local copies, waits for them, and re-layouts: 1.32 us -> 4.07 us
    all_gather x3 -> x0, waiting for transfers between devices: 89.9 us -> none  [the longest x1 48.6 us: per_device(): lax.all_gather(third_context_weight, 'rows', axis=1, tiled=True)]
    pallas_call x0 -> x1, Pallas kernels: none -> 45.4 us  [per_device(): pl.pallas_call(functools.partial(encoder_kernel, n=n, cols=cols, row_pads...]
    all_gather x1 -> x0, blocking collectives: 36.8 us -> none  [per_device(): lax.all_gather(first_context_weight, 'rows', axis=1, tiled=True)]
    ppermute x14 -> x0, starting transfers between devices: 25.4 us -> none  [the longest x7 16.3 us: extended(): before = lax.ppermute(last, axis, up)]
    ppermute x14 -> x0, waiting for transfers between devices: 13.3 us -> none  [the longest x7 13 us: extended(): after = lax.ppermute(leading, axis, down)]
    dot_general x5 -> x0, matrix products: 8.51 us -> none  [tap_product(): jnp.dot(flattened, weight.reshape(channels, weight.shape[-1]), preferred_...]
    broadcast_in_dim x0 -> x3, local copies, waits for them, and re-layouts: none -> 2.43 us  [the longest x1 1.26 us: per_device(): first_b[None]]
  transfers between devices with their start and end apart: 17 -> 0, of which waited for: 10 -> 0; matrix products, arithmetic and copies ran while one was open for 4% -> 0% of each run, Pallas kernels for 0% -> 0%
where the time goes in v1:
time: 50 us; the launch traced here: 49.5 us
  Pallas kernels  45.4 us (91%)
  local copies, waits for them, and re-layouts  4.07 us (8%)
    pallas_call x1, Pallas kernels, per_device(): pl.pallas_call(functools.partial(encoder_kernel, n=n, cols=cols, row_pads...  45.4 us
    unnamed x5, local copies, waits for them, and re-layouts  1.64 us
    broadcast_in_dim x1, local copies, waits for them, and re-layouts, per_device(): first_b[None]  1.26 us

profile of v1, /device:TPU:0, one launch (start us, length us, event | category | flops | bytes accessed | tf_op | source)
XLA Modules:
  0.0 49.5 jit_solution(10404210250333782617)
XLA Ops:
  0.0 0.0 copy-start
  0.0 1.3 %broadcast_in_dim.13.first_b = f32[1,384]{1,0:T(1,128)} reshape(f32[384]{0:T(512)} %param.13) | data formatting | bytes 3072 | tf_op jit(solution)/shard_map/broadcast_in_dim | solution.py:361
  1.3 0.0 copy-done
  1.3 0.0 copy-start.1
  1.3 0.6 %broadcast_in_dim.14.second_b = f32[1,384]{1,0:T(1,128)} reshape(f32[384]{0:T(512)S(1)} %copy-done) | data formatting | bytes 3072 | tf_op jit(solution)/shard_map/broadcast_in_dim | solution.py:361
  1.9 0.1 copy-done.1
  1.9 0.6 %broadcast_in_dim.15.third_b = f32[1,384]{1,0:T(1,128)} reshape(f32[384]{0:T(512)S(1)} %copy-done.1) | data formatting | bytes 3072 | tf_op jit(solution)/shard_map/broadcast_in_dim | solution.py:362
  2.5 45.4 %shard_map.91 = bf16[1,2,64,384]{3,2,1,0:T(8,128)(2,1)} custom-call(bf16[2,2,2,64,128]{4,3,2,1,0:T(8,128)(2,1)} %frames.1, bf16[9,32,512]{2,1,0:T(8,128)(2,1)} %cell_w.1, f32[1,512]{1,0:T(1,128)} %bitcast.1, bf16[9,16,384]{2,1,0:T(8,128)(2,1)} %first_w.1, f32[1,384]{1,0:T(1,128)} %broadcast_in_dim.13.first_b, bf16[9,48,384]{2,1,0:T(8,128)(2,1)} %second_w.1, ...), custom_call_target="tpu_custom_call" | custom-call | tf_op jit(solution)/shard_map/pallas_call | solution.py:336
  47.9 1.5 %copy.11 = bf16[1,2,64,384]{3,2,1,0:T(8,128)(2,1)} copy(bf16[1,2,64,384]{3,2,1,0:T(8,128)(2,1)} %shard_map.91) | data formatting | bytes 196608
Async XLA Ops:
  0.0 1.3 %copy-start = (f32[384]{0:T(512)S(1)}, f32[384]{0:T(512)}, u32[]{:S(2)}) copy-start(f32[384]{0:T(512)} %param.15) | copy-start | bytes 4612
  1.3 0.7 %copy-start.1 = (f32[384]{0:T(512)S(1)}, f32[384]{0:T(512)}, u32[]{:S(2)}) copy-start(f32[384]{0:T(512)} %param.17) | copy-start | bytes 4612

commit v2 on v1

--- a/solution.py
+++ b/solution.py
@@ -13,7 +13,7 @@
 def encoder_kernel(
     frames, cell_w, cell_b, first_w, first_b, second_w, second_b, third_w, third_b,
     out, wc, w1, w2, w3, fp, hp, f1, f2, f3,
-    local_sem, ring_s, ring_r, pair_s, pair_r, ex_s, ex_r, *, n, cols, row_pads,
+    local_sem, ring_s, ring_r, across_s, across_r, pair_s, pair_r, ex_s, ex_r, *, n, cols, shared, row_pads,
 ):
     seg, r, c = lax.axis_index("segment"), lax.axis_index("rows"), lax.axis_index("cols")
     steps, height, across, channels = frames.shape[1:]
@@ -87,6 +87,9 @@
                 barrier, inc=1, device_id=(seg, r + dr, c + dc), device_id_type=MESH_ID
             )
 
+    if shared:
+        expected = expected + 1
+        pl.semaphore_signal(barrier, inc=1, device_id=(1 - seg, r, c), device_id_type=MESH_ID)
     pl.semaphore_wait(barrier, expected)
 
     def exchange(number, source_of, buffer, pad, reach, width):
@@ -143,29 +146,39 @@
         frame_arrivals.append(arrive)
         departs.append(depart)
 
-    def ring_copy(a, k):
-        slot = gathered[a].at[rows_at((place - sign * k + n) % n)]
+    parts = (2 * seg, 1, 2 * (1 - seg)) if shared else (0, 1, 2)
+    carried = range(2) if shared else range(3)
+
+    def slot(a, part, k):
+        span = gathered[a].shape[1] // 3
+        source = rows_at((place - sign * k + n) % n)
+        return gathered[a].at[source, pl.ds(parts[part] * span, span)]
+
+    def ring_copy(a, part, k, sent=True):
+        span = gathered[a].shape[1] // 3
+        place_of = slot(a, part, k if sent else k + 1)
+        start = (9 - 3 * span) // 2 + parts[part] * span
         return pltpu.make_async_remote_copy(
-            src_ref=own[a] if k == 0 else slot,
-            dst_ref=slot,
-            send_sem=ring_s.at[a, k],
-            recv_sem=ring_r.at[a, k],
+            src_ref=stored[a].at[pl.ds(start, span)] if sent and k == 0 else place_of,
+            dst_ref=place_of,
+            send_sem=ring_s.at[a, part, k],
+            recv_sem=ring_r.at[a, part, k],
             device_id=ahead_id,
             device_id_type=MESH_ID,
         )
 
-    def arriving(a, k):
-        slot = gathered[a].at[rows_at((place - sign * k + n) % n)]
+    def across_copy(a, k, sent=True):
+        piece = slot(a, 0 if sent else 2, k)
         return pltpu.make_async_remote_copy(
-            src_ref=slot, dst_ref=slot, send_sem=ring_s.at[a, k - 1],
-            recv_sem=ring_r.at[a, k - 1], device_id=ahead_id, device_id_type=MESH_ID,
-        )
-
-    def pair_copy(a, k, direction):
-        slot = gathered[a].at[rows_at((place - direction * sign * k + n) % n)]
+            src_ref=piece, dst_ref=piece, send_sem=across_s.at[a, k], recv_sem=across_r.at[a, k],
+            device_id=(1 - seg, r, c), device_id_type=MESH_ID,
+        )
+
+    def pair_copy(a, part, k, direction):
+        piece = slot(a, part, direction * k)
         return pltpu.make_async_remote_copy(
-            src_ref=slot, dst_ref=slot, send_sem=pair_s.at[a, k], recv_sem=pair_r.at[a, k],
-            device_id=partner_id, device_id_type=MESH_ID,
+            src_ref=piece, dst_ref=piece, send_sem=pair_s.at[a, part, k],
+            recv_sem=pair_r.at[a, part, k], device_id=partner_id, device_id_type=MESH_ID,
         )
 
     def longer(a):
@@ -177,30 +190,64 @@
         else:
             pl.when(condition)(act)
 
-    def ring_send(a, k):
-        guarded(longer(a) if k == half - 1 else None, ring_copy(a, k).start)
+    def ring_send(a, part, k):
+        guarded(longer(a) if k == half - 1 else None, ring_copy(a, part, k).start)
+
+    def own_send(a):
+        for part in carried:
+            ring_send(a, part, 0)
 
     def ring_step(a, k):
         def act():
-            arriving(a, k).wait_recv()
-            if k < half:
-                ring_send(a, k)
-            pair_copy(a, k, 1).start()
+            for part in carried:
+                ring_copy(a, part, k - 1, False).wait_recv()
+                if k < half:
+                    ring_send(a, part, k)
+                if shared and part == 0:
+                    across_copy(a, k).start()
+                pair_copy(a, part, k, 1).start()
 
         guarded(longer(a) if k == half else None, act)
 
+    def across_step(a, k):
+        def act():
+            across_copy(a, k, False).wait_recv()
+            pair_copy(a, 2, k, 1).start()
+
+        if shared:
+            guarded(longer(a) if k == half else None, act)
+
     def pair_waits(a):
+        shorter = odd_core if a == 0 else even_core
         for k in range(1, half + 1):
-            shorter = odd_core if a == 0 else even_core
-            guarded(shorter if k == half else None, pair_copy(a, k, -1).wait_recv)
-
-    ring_send(0, 0)
+            for part in range(3):
+                guarded(
+                    shorter if k == half else None, pair_copy(a, part, k, -1).wait_recv
+                )
+
+    context_steps = list(range(1, half + 1))
+    quarter = max(1, half // 4)
+
+    def context_ring(count):
+        for _ in range(min(count, len(context_steps))):
+            k = context_steps.pop(0)
+            for a in (1, 2, 3):
+                ring_step(a, k)
+            if k > 1:
+                for a in (1, 2, 3):
+                    across_step(a, k - 1)
+
+    own_send(0)
     for k in range(1, half + 1):
         ring_step(0, k)
+        if k > 1:
+            across_step(0, k - 1)
         if k <= 3:
-            ring_send(k, 0)
+            own_send(k)
     for k in range(half + 1, 4):
-        ring_send(k, 0)
+        own_send(k)
+    context_ring(quarter)
+    across_step(0, half)
 
     for copy in locals_:
         copy.wait()
@@ -208,7 +255,7 @@
         arrive()
     pair_waits(0)
 
-    bias = cell_b[...]
+    bias = cell_b[...].reshape(1, -1)
     per = wc.shape[2]
     frame_sources = channels // per
 
@@ -249,15 +296,6 @@
         memory = fresh if memory is None else forget * memory + fresh
         return (output * jnp.tanh(memory)).astype(jnp.bfloat16), memory
 
-    context_steps = list(range(1, half + 1))
-    quarter = max(1, half // 4)
-
-    def context_ring(count):
-        for _ in range(min(count, len(context_steps))):
-            k = context_steps.pop(0)
-            for a in (1, 2, 3):
-                ring_step(a, k)
-
     seen, unseen = range(frame_sources), range(frame_sources, n)
     hidden, memory = update(gate_part(fp.at[0], seen) + bias, None)
     for t in range(1, steps):
@@ -289,6 +327,8 @@
         departs.append(depart)
         if i == 0:
             context_ring(len(context_steps))
+            for a in (1, 2, 3):
+                across_step(a, half)
         pair_waits(i + 1)
         arrive()
         total = None
@@ -300,7 +340,7 @@
             right = jnp.concatenate([weight[s, t] for s in range(n)], axis=0)
             product = jnp.dot(left, right, preferred_element_type=jnp.float32)
             total = product if total is None else total + product
-        result = jnp.maximum(total + offset[...], 0.0)
+        result = jnp.maximum(total + offset[...].reshape(1, -1), 0.0)
         if i < 2:
             feature = result.astype(jnp.bfloat16)
     context = (feature.astype(jnp.float32) + result).astype(jnp.bfloat16)
@@ -310,12 +350,18 @@
         depart()
     for a in range(4):
         for k in range(half):
-            guarded(longer(a) if k == half - 1 else None, ring_copy(a, k).wait_send)
+            for part in carried:
+                guarded(
+                    longer(a) if k == half - 1 else None, ring_copy(a, part, k).wait_send
+                )
         for k in range(1, half + 1):
-            guarded(longer(a) if k == half else None, pair_copy(a, k, 1).wait_send)
-
-
-def per_device(n, cols, *args):
+            for part in range(3):
+                guarded(longer(a) if k == half else None, pair_copy(a, part, k, 1).wait_send)
+            if shared:
+                guarded(longer(a) if k == half else None, across_copy(a, k).wait_send)
+
+
+def per_device(n, cols, shared, *args):
     import functools
 
     frames, cell_w, cell_b, first_w, first_b, second_w, second_b, third_w, third_b = args
@@ -334,7 +380,7 @@
     dma = pltpu.SemaphoreType.DMA
     anywhere, vmem = pl.BlockSpec(memory_space=pl.ANY), pl.BlockSpec(memory_space=pltpu.VMEM)
     return pl.pallas_call(
-        functools.partial(encoder_kernel, n=n, cols=cols, row_pads=row_pads),
+        functools.partial(encoder_kernel, n=n, cols=cols, shared=shared, row_pads=row_pads),
         out_shape=jax.ShapeDtypeStruct((1, height, across, width), jnp.bfloat16),
         in_specs=[anywhere, anywhere, vmem, anywhere, vmem, anywhere, vmem, anywhere, vmem],
         out_specs=vmem,
@@ -349,17 +395,19 @@
             field(DILATIONS[1], row_pads[1], width),
             field(DILATIONS[2], row_pads[2], width),
             dma((steps + 4,)),
-            dma((4, half)),
-            dma((4, half)),
+            dma((4, 3, half)),
+            dma((4, 3, half)),
             dma((4, half + 1)),
             dma((4, half + 1)),
+            dma((4, 3, half + 1)),
+            dma((4, 3, half + 1)),
             dma((exchanges, 9)),
             dma((exchanges, 9)),
         ],
         compiler_params=pltpu.CompilerParams(collective_id=0, has_side_effects=True),
     )(
-        frames, cell_w, cell_b[None], first_w, first_b[None], second_w, second_b[None],
-        third_w, third_b[None],
+        frames, cell_w, cell_b, first_w, first_b, second_w, second_b,
+        third_w, third_b,
     )
 
 
@@ -372,7 +420,7 @@
         kernels, P(), kernels, P(), kernels, P(), kernels, P(),
     )
     return jax.shard_map(
-        functools.partial(per_device, mesh.shape["rows"], mesh.shape["cols"]),
+        functools.partial(per_device, mesh.shape["rows"], mesh.shape["cols"], mesh.shape["segment"] == 2),
         mesh=mesh,
         in_specs=placed,
         out_specs=P("segment", "rows", "cols", None),

time: 50 us -> 41.6 us (0.83)
  Pallas kernels: 45.4 us -> 39.9 us
  local copies, waits for them, and re-layouts: 4.07 us -> 1.54 us
    pallas_call x1, Pallas kernels: 45.4 us -> 39.9 us  [per_device(): pl.pallas_call(functools.partial(encoder_kernel, n=n, cols=cols, shared=s...]
    broadcast_in_dim x3 -> x0, local copies, waits for them, and re-layouts: 2.43 us -> none  [the longest x1 1.26 us: per_device(): first_b[None]]
    unnamed x5 -> x1, local copies, waits for them, and re-layouts: 1.64 us -> 1.54 us
where the time goes in v2:
time: 41.6 us; the launch traced here: 41.4 us
  Pallas kernels  39.9 us (96%)
  local copies, waits for them, and re-layouts  1.54 us (4%)
    pallas_call x1, Pallas kernels, per_device(): pl.pallas_call(functools.partial(encoder_kernel, n=n, cols=cols, shared=s...  39.9 us
    unnamed x1, local copies, waits for them, and re-layouts  1.54 us

profile of v2, /device:TPU:0, one launch (start us, length us, event | category | flops | bytes accessed | tf_op | source)
XLA Modules:
  0.0 41.4 jit_solution(7534799525074950200)
XLA Ops:
  0.0 39.9 %shard_map.91 = bf16[1,2,64,384]{3,2,1,0:T(8,128)(2,1)} custom-call(bf16[2,2,2,64,128]{4,3,2,1,0:T(8,128)(2,1)} %frames.1, bf16[9,32,512]{2,1,0:T(8,128)(2,1)} %cell_w.1, f32[512]{0:T(512)} %cell_b.1, bf16[9,16,384]{2,1,0:T(8,128)(2,1)} %first_w.1, f32[384]{0:T(512)} %first_b.1, bf16[9,48,384]{2,1,0:T(8,128)(2,1)} %second_w.1, f32[384]{0:T(512)} %second_b.1, ...), custom_call_target="tpu_custom_call" | custom-call | tf_op jit(solution)/shard_map/pallas_call | solution.py:382
  39.9 1.5 %copy.11 = bf16[1,2,64,384]{3,2,1,0:T(8,128)(2,1)} copy(bf16[1,2,64,384]{3,2,1,0:T(8,128)(2,1)} %shard_map.91) | data formatting | bytes 196608

commit v3 on v2

--- a/solution.py
+++ b/solution.py
@@ -19,18 +19,19 @@
     steps, height, across, channels = frames.shape[1:]
     state = cell_b.shape[-1] // 4
     half = n // 2
-    odd = c % 2
+    odd = lax.rem(c, 2)
     even_core, odd_core = odd == 0, odd == 1
     sign = 1 - 2 * odd
-    parity = r % 2
-    place = (1 - parity) * (r // 2) + parity * (n - 1 - r // 2)
+    parity, pair = lax.rem(r, 2), lax.div(r, 2)
+    place = pair + parity * (n - 1 - 2 * pair)
 
     def rows_at(position):
-        upper = position // half
-        return (1 - upper) * 2 * position + upper * (2 * (n - 1 - position) + 1)
-
-    following = rows_at((place + sign + n) % n)
-    preceding = rows_at((place - sign + n) % n)
+        upper = lax.div(position, half)
+        return 2 * position + upper * (2 * n - 1 - 4 * position)
+
+    behind_rows = [r] + [rows_at(lax.rem(place - sign * k + n, n)) for k in range(1, half + 1)]
+    ahead_rows = [r] + [rows_at(lax.rem(place + sign * k + n, n)) for k in range(1, half + 1)]
+    following, preceding = ahead_rows[1], behind_rows[1]
     partner = c + 1 - 2 * odd
     ahead_id, partner_id = (seg, following, c), (seg, r, partner)
 
@@ -44,6 +45,8 @@
         return jnp.logical_and(
             jnp.logical_and(row >= 0, row < n), jnp.logical_and(col >= 0, col < cols)
         )
+
+    inside = {offset: present(*offset) for offset in offsets}
 
     locals_ = []
     for t in range(steps):
@@ -78,7 +81,7 @@
     for target in (following, preceding):
         pl.semaphore_signal(barrier, inc=1, device_id=(seg, target, c), device_id_type=MESH_ID)
     for dr, dc in offsets:
-        there = present(dr, dc)
+        there = inside[dr, dc]
         expected = expected + there.astype(jnp.int32)
 
         @pl.when(there)
@@ -113,7 +116,7 @@
                 device_id=(seg, r + dr * reach, c + dc),
                 device_id_type=MESH_ID,
             )
-            there, behind = present(dr * reach, dc), present(-dr * reach, -dc)
+            there, behind = inside[dr * reach, dc], inside[-dr * reach, -dc]
             pl.when(there)(copy.start)
             departures.append((there, copy))
             arrivals.append((behind, copy))
@@ -151,7 +154,7 @@
 
     def slot(a, part, k):
         span = gathered[a].shape[1] // 3
-        source = rows_at((place - sign * k + n) % n)
+        source = behind_rows[k] if k >= 0 else ahead_rows[-k]
         return gathered[a].at[source, pl.ds(parts[part] * span, span)]
 
     def ring_copy(a, part, k, sent=True):
@@ -242,10 +245,11 @@
         ring_step(0, k)
         if k > 1:
             across_step(0, k - 1)
-        if k <= 3:
-            own_send(k)
-    for k in range(half + 1, 4):
-        own_send(k)
+        if k == 1:
+            for a in (1, 2, 3):
+                own_send(a)
+        else:
+            context_ring(1)
     context_ring(quarter)
     across_step(0, half)
 

time: 41.6 us -> 40.8 us (0.981)
  Pallas kernels: 39.9 us -> 39 us
    pallas_call x1, Pallas kernels: 39.9 us -> 39 us  [per_device(): pl.pallas_call(functools.partial(encoder_kernel, n=n, cols=cols, shared=s...]
where the time goes in v3:
time: 40.8 us; the launch traced here: 40.6 us
  Pallas kernels  39 us (96%)
  local copies, waits for them, and re-layouts  1.54 us (4%)
    pallas_call x1, Pallas kernels, per_device(): pl.pallas_call(functools.partial(encoder_kernel, n=n, cols=cols, shared=s...  39 us
    unnamed x1, local copies, waits for them, and re-layouts  1.54 us

profile of v3, /device:TPU:0, one launch (start us, length us, event | category | flops | bytes accessed | tf_op | source)
XLA Modules:
  0.0 40.6 jit_solution(14447992382121197203)
XLA Ops:
  0.0 39.0 %shard_map.91 = bf16[1,2,64,384]{3,2,1,0:T(8,128)(2,1)} custom-call(bf16[2,2,2,64,128]{4,3,2,1,0:T(8,128)(2,1)} %frames.1, bf16[9,32,512]{2,1,0:T(8,128)(2,1)} %cell_w.1, f32[512]{0:T(512)} %cell_b.1, bf16[9,16,384]{2,1,0:T(8,128)(2,1)} %first_w.1, f32[384]{0:T(512)} %first_b.1, bf16[9,48,384]{2,1,0:T(8,128)(2,1)} %second_w.1, f32[384]{0:T(512)} %second_b.1, ...), custom_call_target="tpu_custom_call" | custom-call | tf_op jit(solution)/shard_map/pallas_call | solution.py:386
  39.0 1.5 %copy.11 = bf16[1,2,64,384]{3,2,1,0:T(8,128)(2,1)} copy(bf16[1,2,64,384]{3,2,1,0:T(8,128)(2,1)} %shard_map.91) | data formatting | bytes 196608
